TPU v7x, 32 devices: a whole 2x2x4 slice. The times are simulated.
32 devices in a mesh: dp: 8 (over z, y), seq: 4 (over x, core).
Axes of the slice: x: 2, y: 2, z: 4, core: 2. Of those that a mesh axis runs over, the one named last changes fastest.
Arguments:
- hidden: bfloat16 [4096, 8192], P(('dp', 'seq')), may hold values from -24 to 24
- queries: bfloat16 [4096, 1024], P(('dp', 'seq')), may hold values from -32 to 32
- kv_weight: bfloat16 [8192, 256], P(('dp', 'seq')), may hold values from -1 to 1
- dest_device: int32 [4096], P(('dp', 'seq')), may hold values from 0 to 3, as said below
- segment_ids: int32 [8, 512], P('dp'), may hold values from 0 to 3, never falling along the last dimension, each value on 1 to 256 neighbouring positions
Outputs:
- attended: bfloat16 [4096, 1024], P(('dp', 'seq'))
Inputs may be any that keep to these rules, and one draw needn't show every extreme that they name: `dest_device`: within a batch group, the number of tokens that device i of seq packs onto device j depends only on (j - i) mod 4; it is at most 32, exactly 32 for some pair of every group, and every device receives 128 tokens.
All inputs are finite; a program needn't handle non-finite values.
Results may differ from a plain program's by a relative error of at most 0.0058.
Values may be sent and summed in bfloat16 or wider, within the bound.
A program may use at most 64 MiB of HBM per device.

v0:
```python
import jax
import jax.numpy as jnp
from jax import lax
from jax.sharding import PartitionSpec as P

HEAD = 128
GROUP = 8


def shifted(shard, axis, by):
    devices = lax.axis_size(axis)
    pairs = [(i, i + by) for i in range(devices) if 0 <= i + by < devices]
    return lax.ppermute(shard, axis, pairs)


def shards(hidden, queries, kv_weight, dest_device, segment_ids):
    rows_dev = hidden.shape[0]
    width_q = GROUP * HEAD
    seq_count = lax.axis_size("seq")
    mine_index = lax.axis_index("seq")
    slots = rows_dev // 4
    reach = seq_count // 2
    scale = 1.0 / HEAD**0.5
    whole_weight = lax.all_gather(kv_weight, ("dp", "seq"), axis=0, tiled=True)
    kv_sum = jnp.dot(hidden, whole_weight, preferred_element_type=jnp.float32)
    kv_vals = kv_sum.astype(jnp.bfloat16)
    feats = jnp.concatenate([queries, kv_vals], axis=1)
    lanes = jnp.arange(seq_count, dtype=jnp.int32)
    offsets = (dest_device - mine_index) % seq_count
    member = (offsets[:, None] == lanes[None, :]).astype(jnp.int32)
    counts = jnp.sum(member, axis=0)
    dest_member = (dest_device[:, None] == lanes[None, :]).astype(jnp.int32)
    rank_in = jnp.sum((jnp.cumsum(dest_member, axis=0) - 1) * dest_member, axis=1)
    send_slot = dest_device * slots + rank_in
    select = (jnp.arange(seq_count * slots, dtype=jnp.int32)[:, None] == send_slot[None, :]).astype(
        jnp.bfloat16
    )
    outgoing = jnp.dot(select, feats, preferred_element_type=jnp.float32).astype(jnp.bfloat16)
    outgoing = outgoing.reshape(seq_count, slots, feats.shape[1])
    received = lax.all_to_all(outgoing, "seq", split_axis=0, concat_axis=0, tiled=True).reshape(
        seq_count * slots, feats.shape[1]
    )
    lookup = ((mine_index - lanes) % seq_count)[:, None] == lanes[None, :]
    from_count = jnp.sum(jnp.where(lookup, counts[None, :], 0), axis=1)
    from_start = jnp.cumsum(from_count) - from_count
    slot_index = jnp.broadcast_to(jnp.arange(slots, dtype=jnp.int32)[None, :], (seq_count, slots))
    dest_pos = (from_start[:, None] + slot_index).reshape(-1)
    valid = (slot_index < from_count[:, None]).reshape(-1)
    placer = (
        (jnp.arange(rows_dev, dtype=jnp.int32)[:, None] == dest_pos[None, :]) & valid[None, :]
    ).astype(jnp.bfloat16)
    packed = jnp.dot(placer, received, preferred_element_type=jnp.float32).astype(jnp.bfloat16)
    query_rows = packed[:, :width_q].reshape(rows_dev, GROUP, HEAD)
    kv_local = packed[:, width_q:]
    seg_row = segment_ids[0]
    own_start = mine_index * rows_dev
    query_seg = lax.dynamic_slice_in_dim(seg_row, own_start, rows_dev, 0)
    query_pos = own_start + jnp.arange(rows_dev, dtype=jnp.int32)

    def attend(carry, piece, start):
        top_old, total_old, numer_old = carry
        count_keys = piece.shape[0]
        key_pos = start + jnp.arange(count_keys, dtype=jnp.int32)
        key_seg = lax.dynamic_slice_in_dim(seg_row, jnp.maximum(start, 0), count_keys, 0)
        allow = (
            (query_seg[:, None] == key_seg[None, :])
            & (key_pos[None, :] <= query_pos[:, None])
            & (key_pos[None, :] >= 0)
        )
        allow = allow[None, :, :]
        scores = (
            jnp.einsum(
                "rgh,kh->grk", query_rows, piece[:, :HEAD], preferred_element_type=jnp.float32
            )
            * scale
        )
        top_new = jnp.maximum(top_old, jnp.max(jnp.where(allow, scores, -1e30), axis=-1))
        weights = jnp.where(allow, jnp.exp(scores - top_new[:, :, None]), 0.0)
        factor = jnp.exp(top_old - top_new)
        total_new = total_old * factor + jnp.sum(weights, axis=-1)
        contrib = jnp.einsum(
            "grk,kh->grh",
            weights.astype(jnp.bfloat16),
            piece[:, HEAD:],
            preferred_element_type=jnp.float32,
        )
        numer_new = numer_old * factor[:, :, None] + contrib
        return (top_new, total_new, numer_new)

    start_carry = (
        jnp.full((GROUP, rows_dev), -1e30, jnp.float32),
        jnp.zeros((GROUP, rows_dev), jnp.float32),
        jnp.zeros((GROUP, rows_dev, HEAD), jnp.float32),
    )
    state = attend(start_carry, kv_local, own_start)
    for back in range(1, reach + 1):
        earlier = shifted(kv_local, "seq", back)
        state = attend(state, earlier, own_start - back * rows_dev)
    top_val, total, numer = state
    result = (numer / total[:, :, None]).astype(jnp.bfloat16)
    return jnp.transpose(result, (1, 0, 2)).reshape(rows_dev, width_q)


def solution(mesh):
    in_specs = (
        P(("dp", "seq"), None),
        P(("dp", "seq"), None),
        P(("dp", "seq"), None),
        P(("dp", "seq")),
        P("dp", None),
    )
    out_specs = P(("dp", "seq"), None)
    return jax.shard_map(shards, mesh=mesh, in_specs=in_specs, out_specs=out_specs, check_vma=False)
```

profile of v0, /device:TPU:1, one launch (start us, length us, event | category | flops | bytes accessed | tf_op | source)
XLA Modules:
  0.0 103.0 jit_solution(13617077591437774022)
XLA Ops:
  6.5 0.0 copy-start
  6.5 0.0 copy-start.1
  6.5 0.0 all-gather.2.cloned.1.call-start
  6.5 0.7 all-gather.2.cloned.1.call-update
  7.3 0.7 fusion.37
  8.0 0.2 reduce_window_sum.18
  8.2 0.8 select_reduce_fusion.3
  9.0 0.7 and_select_fusion
  9.7 0.1 convert_reduce_fusion
  9.8 0.2 select_reduce_fusion.4
  10.0 0.2 reduce-window.8
  10.2 0.9 fusion.51
  11.1 0.1 iota_compare_fusion.4
  11.2 0.1 iota_add_fusion
  11.3 63.1 %all-gather.2.cloned.1.call-done = bf16[8192,256]{1,0:T(8,128)(2,1)} async-done(((bf16[256,256]{1,0:T(8,128)(2,1)}), bf16[8192,256]{1,0:T(8,128)(2,1)}) %all-gather.2.cloned.1.call-update) | async-done | bytes 4194320 | tf_op jit(solution)/shard_map/all_gather | solution.py:24
  74.4 0.0 copy-done
  74.4 2.9 %convolution_convert_fusion.2 = bf16[128,256]{1,0:T(8,128)(2,1)S(1)} fusion(bf16[128,8192]{1,0:T(8,128)(2,1)S(1)} %copy-done, bf16[8192,256]{1,0:T(8,128)(2,1)} %all-gather.2.cloned.1.call-done), kind=kOutput, calls=%fused_computation.18 | convolution fusion | flops 536903680 | bytes 6356992 | tf_op jit(solution)/shard_map/dot_general | solution.py:25
  77.3 0.0 copy-done.1
  77.3 1.0 convolution_convert_fusion.1
  78.3 3.7 %all-to-all-start = ((bf16[4,32,1280]{2,1,0:T(8,128)(2,1)}), bf16[4,32,1280]{2,1,0:T(8,128)(2,1)S(1)}, u32[]{:S(2)}, u32[]{:S(2)}) async-start(bf16[4,32,1280]{2,1,0:T(8,128)(2,1)} %bitcast.4), calls=%async_computation | async-start | bytes 655360 | tf_op jit(solution)/shard_map/all_to_all | solution.py:40
  82.0 0.1 lt.38
  82.1 0.1 add.131
  82.1 0.2 and_and_fusion
  82.4 5.3 %all-to-all-done = bf16[4,32,1280]{2,1,0:T(8,128)(2,1)S(1)} async-done(((bf16[4,32,1280]{2,1,0:T(8,128)(2,1)}), bf16[4,32,1280]{2,1,0:T(8,128)(2,1)S(1)}, u32[]{:S(2)}, u32[]{:S(2)}) %all-to-all-start) | async-done | bytes 327712 | tf_op jit(solution)/shard_map/all_to_all | solution.py:40
  87.7 0.2 convolution_convert_fusion
  88.0 2.4 %collective-permute-start.1 = (bf16[128,256]{1,0:T(8,128)(2,1)S(1)}, bf16[128,256]{1,0:T(8,128)(2,1)S(1)}, u32[]{:S(2)}, u32[]{:S(2)}) collective-permute-start(bf16[128,256]{1,0:T(8,128)(2,1)S(1)} %slice.37), channel_id=1, source_target_pairs={{0,2},{1,3},{4,6},{5,7},{8,10},{9,11},{12,14},{13,15},{16,18},{17,... | collective-permute-start | bytes 196616 | tf_op jit(solution)/shard_map/ppermute | solution.py:13
  90.4 1.9 %collective-permute-start = (bf16[128,256]{1,0:T(8,128)(2,1)S(1)}, bf16[128,256]{1,0:T(8,128)(2,1)S(1)}, u32[]{:S(2)}, u32[]{:S(2)}) collective-permute-start(bf16[128,256]{1,0:T(8,128)(2,1)S(1)} %slice.37), channel_id=1, source_target_pairs={{0,1},{1,2},{2,3},{4,5},{5,6},{6,7},{8,9},{9,10},{10,11},{12,13},{... | collective-permute-start | bytes 196616 | tf_op jit(solution)/shard_map/ppermute | solution.py:13
  92.3 0.2 select_reduce_fusion.2
  92.5 1.1 %collective-permute-done = bf16[128,256]{1,0:T(8,128)(2,1)S(1)} collective-permute-done((bf16[128,256]{1,0:T(8,128)(2,1)S(1)}, bf16[128,256]{1,0:T(8,128)(2,1)S(1)}, u32[]{:S(2)}, u32[]{:S(2)}) %collective-permute-start) | collective-permute-done | bytes 65568 | tf_op jit(solution)/shard_map/ppermute | solution.py:13
  93.6 0.2 select_reduce_fusion.1
  93.8 0.0 collective-permute-done.1
  93.9 0.2 select_reduce_fusion
  94.1 0.1 fusion.14
  94.2 0.1 fusion.12
  94.3 0.1 fusion.10
  94.5 0.3 fusion.6
  94.8 0.3 fusion.7
  95.0 0.3 fusion.9
  95.3 0.9 copy.25
  (9 shorter events, 0.1 us)
Async XLA Ops:
  6.5 67.9 %copy-start = (bf16[128,8192]{1,0:T(8,128)(2,1)S(1)}, bf16[128,8192]{1,0:T(8,128)(2,1)}, u32[]{:S(2)}) copy-start(bf16[128,8192]{1,0:T(8,128)(2,1)} %param.5) | copy-start | bytes 6291460
  6.5 70.8 %copy-start.1 = (bf16[128,1024]{1,0:T(8,128)(2,1)S(1)}, bf16[128,1024]{1,0:T(8,128)(2,1)}, u32[]{:S(2)}) copy-start(bf16[128,1024]{1,0:T(8,128)(2,1)} %param.6) | copy-start | bytes 786436
  6.5 67.9 %all-gather.2.cloned.1.call-start = ((), (), s32[]{:S(2)}) async-start(), calls=%async_computation.1 | async-start | bytes 4325376 | tf_op jit(solution)/shard_map/all_gather | solution.py:24
  78.3 9.4 %all-to-all-start = ((bf16[4,32,1280]{2,1,0:T(8,128)(2,1)}), bf16[4,32,1280]{2,1,0:T(8,128)(2,1)S(1)}, u32[]{:S(2)}, u32[]{:S(2)}) async-start(bf16[4,32,1280]{2,1,0:T(8,128)(2,1)} %bitcast.4), calls=%async_computation | async-start | bytes 655360 | tf_op jit(solution)/shard_map/all_to_all | solution.py:40
  88.0 5.9 %collective-permute-start.1 = (bf16[128,256]{1,0:T(8,128)(2,1)S(1)}, bf16[128,256]{1,0:T(8,128)(2,1)S(1)}, u32[]{:S(2)}, u32[]{:S(2)}) collective-permute-start(bf16[128,256]{1,0:T(8,128)(2,1)S(1)} %slice.37), channel_id=1, source_target_pairs={{0,2},{1,3},{4,6},{5,7},{8,10},{9,11},{12,14},{13,15},{16,18},{17,... | collective-permute-start | bytes 196616 | tf_op jit(solution)/shard_map/ppermute | solution.py:13
  90.4 3.2 %collective-permute-start = (bf16[128,256]{1,0:T(8,128)(2,1)S(1)}, bf16[128,256]{1,0:T(8,128)(2,1)S(1)}, u32[]{:S(2)}, u32[]{:S(2)}) collective-permute-start(bf16[128,256]{1,0:T(8,128)(2,1)S(1)} %slice.37), channel_id=1, source_target_pairs={{0,1},{1,2},{2,3},{4,5},{5,6},{6,7},{8,9},{9,10},{10,11},{12,13},{... | collective-permute-start | bytes 196616 | tf_op jit(solution)/shard_map/ppermute | solution.py:13
Sparse Core Ops, SparseCore 0:
  10.2 64.1 all-gather.1
where the time goes:
time: 103 us
  waiting for transfers between devices  70.3 us (68%)
  between operations  13.6 us (13%)
  starting transfers between devices  7.98 us (8%)
  matrix products  5.61 us (5%)
  other arithmetic  3.63 us (4%)
  local copies, waits for them, and re-layouts  1.95 us (2%)
    all_gather x1, waiting for transfers between devices, shards(): whole_weight = lax.all_gather(kv_weight, ('dp', 'seq'), axis=0, tiled=True)  63.1 us
    all_to_all x1, waiting for transfers between devices, shards(): lax.all_to_all(outgoing, 'seq', split_axis=0, concat_axis=0, tiled=True)  5.34 us
    ppermute x2, starting transfers between devices, shifted(): return lax.ppermute(shard, axis, pairs)  4.3 us
    all_to_all x1, starting transfers between devices, shards(): lax.all_to_all(outgoing, 'seq', split_axis=0, concat_axis=0, tiled=True)  3.68 us
    dot_general x1, matrix products, shards(): kv_sum = jnp.dot(hidden, whole_weight, preferred_element_type=jnp.float32)  2.9 us
  transfers between devices with their start and end apart: 4, of which 3 were waited for; matrix products, arithmetic and copies ran while one was open for 5% of the time, Pallas kernels for 0%

commit v1 on v0

--- a/solution.py
+++ b/solution.py
@@ -1,10 +1,16 @@
+import functools
+
 import jax
 import jax.numpy as jnp
 from jax import lax
+from jax.experimental import pallas as pl
+from jax.experimental.pallas import tpu as pltpu
 from jax.sharding import PartitionSpec as P
 
 HEAD = 128
 GROUP = 8
+PIECES = 1
+MESH = pl.DeviceIdType.MESH
 
 
 def shifted(shard, axis, by):
@@ -101,6 +107,315 @@
     return jnp.transpose(result, (1, 0, 2)).reshape(rows_dev, width_q)
 
 
+def fused(
+    nz, ny, nx, hid_hbm, qry_hbm, w_hbm, dest_ref, seg_ref, out_ref,
+    hid, qry, wbuf, outgoing, received, dest_all, kv_all, packed, bias, acc,
+    load_sem, w_send, w_recv, small_send, dest_recv, qry_recv, kv_recv,
+):
+    rows = hid.shape[0]
+    depth = wbuf.shape[1]
+    n_seq = nx * 2
+    slots = rows // 4
+    keys = n_seq * rows
+    group = lax.axis_index("dp")
+    me = lax.axis_index("seq")
+    z, y = lax.div(group, ny), lax.rem(group, ny)
+    x, c = lax.div(me, 2), lax.rem(me, 2)
+    x1, y1 = x + (1 - c) * (1 - 2 * x), y + c * (1 - 2 * y)
+    x3, y3 = x + c * (1 - 2 * x), y + (1 - c) * (1 - 2 * y)
+    xo, yo = 1 - x, 1 - y
+
+    def dev(zz, yy, xx, cc):
+        return (zz * ny + yy, xx * 2 + cc)
+
+    def block_of(zz, yy, xx, cc):
+        return (zz * ny + yy) * n_seq + xx * 2 + cc
+
+    first, third = dev(z, y1, x1, c), dev(z, y3, x3, c)
+    partner = dev(z, y, x, 1 - c)
+    peers = [lax.rem(me + i, n_seq) for i in range(1, n_seq)]
+
+    mine = block_of(z, y, x, c)
+    load_q = pltpu.make_async_copy(qry_hbm, qry, load_sem.at[0])
+    load_w = pltpu.make_async_copy(w_hbm, wbuf.at[mine], load_sem.at[1])
+    load_h = pltpu.make_async_copy(hid_hbm, hid, load_sem.at[2])
+    load_q.start()
+    load_w.start()
+    load_h.start()
+
+    barrier = pltpu.get_barrier_semaphore()
+    for peer in peers:
+        pl.semaphore_signal(barrier, inc=1, device_id=(group, peer), device_id_type=MESH)
+    pl.semaphore_signal(barrier, inc=1, device_id=dev(z, yo, x, c), device_id_type=MESH)
+
+    @pl.when(z > 0)
+    def _():
+        pl.semaphore_signal(barrier, inc=1, device_id=dev(z - 1, y, x, c), device_id_type=MESH)
+
+    @pl.when(z < nz - 1)
+    def _():
+        pl.semaphore_signal(barrier, inc=1, device_id=dev(z + 1, y, x, c), device_id_type=MESH)
+
+    above, below = (z < nz - 1).astype(jnp.int32), (z > 0).astype(jnp.int32)
+    pl.semaphore_wait(barrier, n_seq + above + below)
+
+    pending = []
+    count = [0]
+
+    def small(src, dst, recv, where, number):
+        copy = pltpu.make_async_remote_copy(
+            src_ref=src, dst_ref=dst, send_sem=small_send.at[number], recv_sem=recv,
+            device_id=where, device_id_type=MESH,
+        )
+        copy.start()
+        pending.append((None, copy))
+
+    for i, peer in enumerate(peers):
+        small(dest_ref, dest_all.at[me], dest_recv.at[me], (group, peer), i)
+
+    piece = depth // PIECES
+
+    def part(ref, j):
+        return ref.at[pl.ds(j * piece, piece), :]
+
+    def send(src, block, j, where, cond=None):
+        number = count[0]
+        count[0] += 1
+        copy = pltpu.make_async_remote_copy(
+            src_ref=part(src, j), dst_ref=part(wbuf.at[block], j),
+            send_sem=w_send.at[number], recv_sem=w_recv.at[block, j],
+            device_id=where, device_id_type=MESH,
+        )
+        pending.append((cond, copy))
+        if cond is None:
+            copy.start()
+        else:
+            pl.when(cond)(copy.start)
+
+    def arrive(block, j):
+        pltpu.make_async_remote_copy(
+            src_ref=part(wbuf.at[block], j), dst_ref=part(wbuf.at[block], j),
+            send_sem=w_send.at[0], recv_sem=w_recv.at[block, j],
+            device_id=partner, device_id_type=MESH,
+        ).wait_recv()
+
+    def multiply(block):
+        columns = pl.ds(pl.multiple_of(block * depth, depth), depth)
+        acc[...] += jnp.dot(hid[:, columns], wbuf[block], preferred_element_type=jnp.float32)
+
+    def origin(k):
+        low = jnp.minimum(z, nz - 1 - z)
+        near = z - 1 - k // 2 if k % 2 == 0 else z + 1 + k // 2
+        rest = jnp.where(z == low, k + 1, nz - 2 - k)
+        return jnp.where(k < 2 * low, near, rest)
+
+    units = [(z, True), (z, False)]
+    for k in range(nz - 1):
+        units += [(origin(k), True), (origin(k), False)]
+
+    def take_mine(i):
+        zz, own = units[i]
+        block = block_of(zz, y, x, c) if own else block_of(zz, y1, x1, c)
+        for j in range(PIECES):
+            if i == 0:
+                src = w_hbm
+            else:
+                src = wbuf.at[block]
+                arrive(block, j)
+            if i < 2:
+                up, down = z < nz - 1, z > 0
+                if i == 1 and nz == 2:
+                    up, down = z < 0, z < 0
+                send(src, block, j, dev(jnp.minimum(z + 1, nz - 1), y, x, c), up)
+                send(src, block, j, dev(jnp.maximum(z - 1, 0), y, x, c), down)
+                if i == 0:
+                    send(src, block, j, first)
+            else:
+                ahead = jnp.where(zz < z, z + 1, z - 1)
+                inside = (ahead >= 0) & (ahead <= nz - 1)
+                span = jnp.where(zz < z, z - zz, zz - z)
+                target = jnp.clip(ahead, 0, nz - 1)
+                if own:
+                    send(src, block, j, dev(target, y, x, c), inside)
+                    send(src, block, j, first, span == nz - 1)
+                else:
+                    send(src, block, j, dev(target, y, x, c), inside & (span + 1 < nz - 1))
+            send(src, block, j, third)
+            send(src, block, j, partner)
+        if i == 0:
+            return
+        multiply(block)
+
+    def take_third(i):
+        zz, own = units[i]
+        block = block_of(zz, y3, x3, c) if own else block_of(zz, yo, xo, c)
+        for j in range(PIECES):
+            arrive(block, j)
+            send(wbuf.at[block], block, j, partner)
+        multiply(block)
+
+    def take_partner(i, far):
+        zz, own = units[i]
+        if far:
+            block = block_of(zz, y1, x1, 1 - c) if own else block_of(zz, yo, xo, 1 - c)
+        else:
+            block = block_of(zz, y, x, 1 - c) if own else block_of(zz, y3, x3, 1 - c)
+        for j in range(PIECES):
+            arrive(block, j)
+        multiply(block)
+
+    def column(row):
+        size = row.shape[1]
+        a = lax.broadcasted_iota(jnp.int32, (size, size), 0)
+        b = lax.broadcasted_iota(jnp.int32, (size, size), 1)
+        return jnp.sum(jnp.where(a == b, row, 0.0), axis=1, keepdims=True)
+
+    def send_queries():
+        load_q.wait()
+        row = dest_ref[...].astype(jnp.float32)
+        col = column(row)
+        a = lax.broadcasted_iota(jnp.int32, (rows, rows), 0)
+        b = lax.broadcasted_iota(jnp.int32, (rows, rows), 1)
+        rank = jnp.sum(jnp.where((col == row) & (a < b), 1.0, 0.0), axis=0, keepdims=True)
+        slot = row * slots + rank
+        number = lax.broadcasted_iota(jnp.int32, (n_seq * slots, rows), 0).astype(jnp.float32)
+        select = jnp.where(number == slot, 1.0, 0.0).astype(jnp.bfloat16)
+        moved = jnp.dot(select, qry[...], preferred_element_type=jnp.float32)
+        outgoing[...] = moved.astype(jnp.bfloat16).reshape(outgoing.shape)
+        for i, peer in enumerate(peers):
+            small(outgoing.at[peer], received.at[me], qry_recv.at[me], (group, peer), n_seq + i)
+        dest_all[me] = dest_ref[...]
+        received[me] = outgoing[me]
+
+    def wait_small(buffer, sems):
+        for peer in peers:
+            pltpu.make_async_remote_copy(
+                src_ref=buffer.at[peer], dst_ref=buffer.at[peer], send_sem=small_send.at[0],
+                recv_sem=sems.at[peer], device_id=partner, device_id_type=MESH,
+            ).wait_recv()
+
+    def prepare():
+        wait_small(dest_all, dest_recv)
+        wait_small(received, qry_recv)
+        every = [dest_all[i].astype(jnp.float32) for i in range(n_seq)]
+        row = jnp.concatenate(every, axis=1)
+        a = lax.broadcasted_iota(jnp.int32, (rows, keys), 0)
+        b = lax.broadcasted_iota(jnp.int32, (rows, keys), 1)
+        position = jnp.zeros((1, keys), jnp.float32)
+        for i in range(n_seq):
+            col = column(every[i])
+            before = (col < row) | ((col == row) & (a + i * rows < b))
+            position += jnp.sum(jnp.where(before, 1.0, 0.0), axis=0, keepdims=True)
+        segment = seg_ref[...].astype(jnp.float32)
+        own_pos = a + me * rows
+        own_seg = jnp.sum(jnp.where(own_pos == b, segment, 0.0), axis=1, keepdims=True)
+        low = jnp.sum(jnp.where(segment < own_seg, 1.0, 0.0), axis=1, keepdims=True)
+        allow = (position >= low) & (position <= own_pos.astype(jnp.float32))
+        bias[...] = jnp.where(allow, 0.0, -1e30)
+        width = n_seq * slots
+        lane = lax.broadcasted_iota(jnp.int32, (1, width), 1)
+        start = jnp.zeros((1, 1), jnp.float32)
+        target = jnp.zeros((1, width), jnp.float32)
+        mine_f = me.astype(jnp.float32)
+        for i in range(n_seq):
+            amount = jnp.sum(jnp.where(every[i] == mine_f, 1.0, 0.0), axis=1, keepdims=True)
+            slot = (lane - i * slots).astype(jnp.float32)
+            inside = (slot >= 0.0) & (slot < slots)
+            target = jnp.where(inside, jnp.where(slot < amount, start + slot, -1.0), target)
+            start = start + amount
+        place_row = lax.broadcasted_iota(jnp.int32, (rows, width), 0).astype(jnp.float32)
+        placer = jnp.where(place_row == target, 1.0, 0.0).astype(jnp.bfloat16)
+        arrived = received[...].reshape(width, GROUP * HEAD)
+        packed[...] = jnp.dot(placer, arrived, preferred_element_type=jnp.float32).astype(jnp.bfloat16)
+
+    acc[...] = jnp.zeros_like(acc)
+    last = len(units)
+    for i in range(last + 2):
+        if i < last:
+            take_mine(i)
+        if i == 0:
+            send_queries()
+            load_w.wait()
+            load_h.wait()
+            multiply(mine)
+        if i == 3:
+            prepare()
+        if 0 <= i - 1 < last:
+            take_third(i - 1)
+            take_partner(i - 1, False)
+        if 0 <= i - 2 < last:
+            take_partner(i - 2, True)
+
+    kv_all[me] = acc[...].astype(jnp.bfloat16)
+    for i, peer in enumerate(peers):
+        small(kv_all.at[me], kv_all.at[me], kv_recv.at[me], (group, peer), 2 * n_seq + i)
+    wait_small(kv_all, kv_recv)
+
+    scale = 1.0 / HEAD**0.5
+    key = kv_all[:, :, :HEAD].reshape(keys, HEAD)
+    value = kv_all[:, :, HEAD:].reshape(keys, HEAD)
+    for h in range(GROUP):
+        cols = pl.ds(h * HEAD, HEAD)
+        scores = lax.dot_general(
+            packed[:, cols], key, (((1,), (1,)), ((), ())), preferred_element_type=jnp.float32
+        )
+        scores = scores * scale + bias[...]
+        top = jnp.max(scores, axis=1, keepdims=True)
+        weights = jnp.exp(scores - top)
+        total = jnp.sum(weights, axis=1, keepdims=True)
+        numer = jnp.dot(weights.astype(jnp.bfloat16), value, preferred_element_type=jnp.float32)
+        out_ref[:, cols] = (numer / total).astype(jnp.bfloat16)
+
+    for cond, copy in pending:
+        if cond is None:
+            copy.wait_send()
+        else:
+            pl.when(cond)(copy.wait_send)
+
+
+def fused_shards(hidden, queries, kv_weight, dest_device, segment_ids):
+    n_seq, n_dp = lax.axis_size("seq"), lax.axis_size("dp")
+    ny, nx = 2, n_seq // 2
+    nz = n_dp // ny
+    rows, d_model = hidden.shape
+    depth, width = kv_weight.shape
+    blocks = n_dp * n_seq
+    width_q = queries.shape[1]
+    keys = n_seq * rows
+    dma = pltpu.SemaphoreType.DMA
+    anyspace = pl.BlockSpec(memory_space=pl.ANY)
+    vmem = pl.BlockSpec(memory_space=pltpu.VMEM)
+    bf16, f32 = jnp.bfloat16, jnp.float32
+    return pl.pallas_call(
+        functools.partial(fused, nz, ny, nx),
+        out_shape=jax.ShapeDtypeStruct((rows, width_q), bf16),
+        in_specs=[anyspace, anyspace, anyspace, vmem, vmem],
+        out_specs=vmem,
+        scratch_shapes=[
+            pltpu.VMEM((rows, d_model), bf16),
+            pltpu.VMEM((rows, width_q), bf16),
+            pltpu.VMEM((blocks, depth, width), bf16),
+            pltpu.VMEM((n_seq, rows // 4, width_q), bf16),
+            pltpu.VMEM((n_seq, rows // 4, width_q), bf16),
+            pltpu.VMEM((n_seq, 1, rows), jnp.int32),
+            pltpu.VMEM((n_seq, rows, width), bf16),
+            pltpu.VMEM((rows, width_q), bf16),
+            pltpu.VMEM((rows, keys), f32),
+            pltpu.VMEM((rows, width), f32),
+            dma((3,)),
+            dma((PIECES * (9 + 9 * nz),)),
+            dma((blocks, PIECES)),
+            dma((3 * n_seq,)),
+            dma((n_seq,)),
+            dma((n_seq,)),
+            dma((n_seq,)),
+        ],
+        compiler_params=pltpu.CompilerParams(
+            collective_id=0, has_side_effects=True, vmem_limit_bytes=32 * 1024 * 1024
+        ),
+    )(hidden, queries, kv_weight, dest_device.reshape(1, rows), segment_ids)
+
+
 def solution(mesh):
     in_specs = (
         P(("dp", "seq"), None),
@@ -110,4 +425,6 @@
         P("dp", None),
     )
     out_specs = P(("dp", "seq"), None)
-    return jax.shard_map(shards, mesh=mesh, in_specs=in_specs, out_specs=out_specs, check_vma=False)
+    n_dp, n_seq = mesh.shape["dp"], mesh.shape["seq"]
+    body = fused_shards if n_seq == 4 and n_dp % 2 == 0 and 4 <= n_dp <= 16 else shards
+    return jax.shard_map(body, mesh=mesh, in_specs=in_specs, out_specs=out_specs, check_vma=False)

time: 103 us -> 47.8 us (0.46)
  waiting for transfers between devices: 70.3 us -> 0 us
  Pallas kernels: 0 us -> 42.1 us
  between operations: 13.6 us -> 0.01 us
  starting transfers between devices: 7.98 us -> 0 us
  matrix products: 5.61 us -> 0 us
  other arithmetic: 3.63 us -> 0 us
  local copies, waits for them, and re-layouts: 1.95 us -> 5.48 us
    all_gather x1 -> x0, waiting for transfers between devices: 63.1 us -> none  [shards(): whole_weight = lax.all_gather(kv_weight, ('dp', 'seq'), axis=0, tiled=True)]
    pallas_call x0 -> x1, Pallas kernels: none -> 42.1 us  [fused_shards(): pl.pallas_call(functools.partial(fused, nz, ny, nx), out_shape=jax.ShapeD...]
    dot_general x9 -> x0, matrix products: 5.61 us -> none  [the longest x1 2.9 us: shards(): kv_sum = jnp.dot(hidden, whole_weight, preferred_element_type=jnp.float32)]
    unnamed x4 -> x11, local copies, waits for them, and re-layouts: 0.01 us -> 5.48 us
    all_to_all x1 -> x0, waiting for transfers between devices: 5.34 us -> none  [shards(): lax.all_to_all(outgoing, 'seq', split_axis=0, concat_axis=0, tiled=True)]
    ppermute x2 -> x0, starting transfers between devices: 4.3 us -> none  [shifted(): return lax.ppermute(shard, axis, pairs)]
    all_to_all x1 -> x0, starting transfers between devices: 3.68 us -> none  [shards(): lax.all_to_all(outgoing, 'seq', split_axis=0, concat_axis=0, tiled=True)]
    reduce_sum x6 -> x0, other arithmetic: 1.44 us -> none  [the longest x1 0.82 us: shards(): jnp.sum((jnp.cumsum(dest_member, axis=0) - 1) * dest_member, axis=1)]
  transfers between devices with their start and end apart: 4 -> 0, of which waited for: 3 -> 0; matrix products, arithmetic and copies ran while one was open for 5% -> 0% of each run, Pallas kernels for 0% -> 0%
where the time goes in v1:
time: 47.8 us; the launch traced here: 47.6 us
  Pallas kernels  42.1 us (88%)
  local copies, waits for them, and re-layouts  5.48 us (11%)
    pallas_call x1, Pallas kernels, fused_shards(): pl.pallas_call(functools.partial(fused, nz, ny, nx), out_shape=jax.ShapeD...  42.1 us
    unnamed x11, local copies, waits for them, and re-layouts  5.48 us

profile of v1, /device:TPU:1, one launch (start us, length us, event | category | flops | bytes accessed | tf_op | source)
XLA Modules:
  0.0 47.6 jit_solution(4789401521418146054)
XLA Ops:
  0.0 0.0 copy-start
  0.0 1.6 %copy-done = bf16[128,8192]{1,0:T(8,128)(2,1)S(1)} copy-done((bf16[128,8192]{1,0:T(8,128)(2,1)S(1)}, bf16[128,8192]{1,0:T(8,128)(2,1)}, u32[]{:S(2)}) %copy-start) | copy-done | bytes 2097176
  1.6 0.0 copy-start.1
  1.6 0.9 %copy-done.1 = bf16[128,1024]{1,0:T(8,128)(2,1)S(1)} copy-done((bf16[128,1024]{1,0:T(8,128)(2,1)S(1)}, bf16[128,1024]{1,0:T(8,128)(2,1)}, u32[]{:S(2)}) %copy-start.1) | copy-done | bytes 262168
  2.5 0.0 copy-start.2
  2.5 0.9 %copy-done.2 = bf16[256,256]{1,0:T(8,128)(2,1)S(1)} copy-done((bf16[256,256]{1,0:T(8,128)(2,1)S(1)}, bf16[256,256]{1,0:T(8,128)(2,1)}, u32[]{:S(2)}) %copy-start.2) | copy-done | bytes 131096
  3.4 0.0 copy-start.3
  3.4 0.7 %copy-done.3 = s32[1,512]{1,0:T(1,128)S(1)} copy-done((s32[1,512]{1,0:T(1,128)S(1)}, s32[1,512]{1,0:T(1,128)}, u32[]{:S(2)}) %copy-start.3) | copy-done | bytes 2072
  4.1 0.0 copy-start.4
  4.1 0.7 %copy-done.4 = s32[128]{0:T(128)S(1)} copy-done((s32[128]{0:T(128)S(1)}, s32[128]{0:T(128)}, u32[]{:S(2)}) %copy-start.4) | copy-done | bytes 536
  4.8 42.1 %shard_map.55 = bf16[128,1024]{1,0:T(8,128)(2,1)S(1)} custom-call(bf16[128,8192]{1,0:T(8,128)(2,1)S(1)} %copy-done, bf16[128,1024]{1,0:T(8,128)(2,1)S(1)} %copy-done.1, bf16[256,256]{1,0:T(8,128)(2,1)S(1)} %copy-done.2, s32[1,128]{1,0:T(1,128)S(1)} %bitcast.1, s32[1,512]{1,0:T(1,128)S(1)} %copy-done.3), custom_call_target="tpu_custom_call" | custom-call | tf_op jit(solution)/shard_map/pallas_call | solution.py:389
  46.9 0.7 %copy.7 = bf16[128,1024]{1,0:T(8,128)(2,1)} copy(bf16[128,1024]{1,0:T(8,128)(2,1)S(1)} %shard_map.55) | data formatting | bytes 524288
Async XLA Ops:
  0.0 1.6 %copy-start = (bf16[128,8192]{1,0:T(8,128)(2,1)S(1)}, bf16[128,8192]{1,0:T(8,128)(2,1)}, u32[]{:S(2)}) copy-start(bf16[128,8192]{1,0:T(8,128)(2,1)} %hid_hbm.1) | copy-start | bytes 6291460
  1.6 0.9 %copy-start.1 = (bf16[128,1024]{1,0:T(8,128)(2,1)S(1)}, bf16[128,1024]{1,0:T(8,128)(2,1)}, u32[]{:S(2)}) copy-start(bf16[128,1024]{1,0:T(8,128)(2,1)} %qry_hbm.1) | copy-start | bytes 786436
  2.5 0.9 %copy-start.2 = (bf16[256,256]{1,0:T(8,128)(2,1)S(1)}, bf16[256,256]{1,0:T(8,128)(2,1)}, u32[]{:S(2)}) copy-start(bf16[256,256]{1,0:T(8,128)(2,1)} %w_hbm.1) | copy-start | bytes 393220
  3.4 0.7 %copy-start.3 = (s32[1,512]{1,0:T(1,128)S(1)}, s32[1,512]{1,0:T(1,128)}, u32[]{:S(2)}) copy-start(s32[1,512]{1,0:T(1,128)} %seg_ref.1) | copy-start | bytes 6148
  4.1 0.7 %copy-start.4 = (s32[128]{0:T(128)S(1)}, s32[128]{0:T(128)}, u32[]{:S(2)}) copy-start(s32[128]{0:T(128)} %param.8) | copy-start | bytes 1540

commit v2 on v1

--- a/solution.py
+++ b/solution.py
@@ -9,7 +9,9 @@
 
 HEAD = 128
 GROUP = 8
-PIECES = 1
+PIECES = 2
+FAR = 2
+LAGS = (2, 2, 3)
 MESH = pl.DeviceIdType.MESH
 
 
@@ -115,6 +117,7 @@
     rows = hid.shape[0]
     depth = wbuf.shape[1]
     n_seq = nx * 2
+    far = FAR
     slots = rows // 4
     keys = n_seq * rows
     group = lax.axis_index("dp")
@@ -224,7 +227,7 @@
                 arrive(block, j)
             if i < 2:
                 up, down = z < nz - 1, z > 0
-                if i == 1 and nz == 2:
+                if i == 1 and far < 2:
                     up, down = z < 0, z < 0
                 send(src, block, j, dev(jnp.minimum(z + 1, nz - 1), y, x, c), up)
                 send(src, block, j, dev(jnp.maximum(z - 1, 0), y, x, c), down)
@@ -237,9 +240,9 @@
                 target = jnp.clip(ahead, 0, nz - 1)
                 if own:
                     send(src, block, j, dev(target, y, x, c), inside)
-                    send(src, block, j, first, span == nz - 1)
+                    send(src, block, j, first, span >= far)
                 else:
-                    send(src, block, j, dev(target, y, x, c), inside & (span + 1 < nz - 1))
+                    send(src, block, j, dev(target, y, x, c), inside & (span + 1 < far))
             send(src, block, j, third)
             send(src, block, j, partner)
         if i == 0:
@@ -330,7 +333,8 @@
 
     acc[...] = jnp.zeros_like(acc)
     last = len(units)
-    for i in range(last + 2):
+    lag_third, lag_near, lag_far = LAGS
+    for i in range(last + max(LAGS)):
         if i < last:
             take_mine(i)
         if i == 0:
@@ -340,11 +344,12 @@
             multiply(mine)
         if i == 3:
             prepare()
-        if 0 <= i - 1 < last:
-            take_third(i - 1)
-            take_partner(i - 1, False)
-        if 0 <= i - 2 < last:
-            take_partner(i - 2, True)
+        if 0 <= i - lag_third < last:
+            take_third(i - lag_third)
+        if 0 <= i - lag_near < last:
+            take_partner(i - lag_near, False)
+        if 0 <= i - lag_far < last:
+            take_partner(i - lag_far, True)
 
     kv_all[me] = acc[...].astype(jnp.bfloat16)
     for i, peer in enumerate(peers):

time: 47.8 us -> 45 us (0.941)
  Pallas kernels: 42.1 us -> 39.2 us
    pallas_call x1, Pallas kernels: 42.1 us -> 39.2 us  [fused_shards(): pl.pallas_call(functools.partial(fused, nz, ny, nx), out_shape=jax.ShapeD...]
where the time goes in v2:
time: 45 us; the launch traced here: 44.7 us
  Pallas kernels  39.2 us (87%)
  local copies, waits for them, and re-layouts  5.48 us (12%)
    pallas_call x1, Pallas kernels, fused_shards(): pl.pallas_call(functools.partial(fused, nz, ny, nx), out_shape=jax.ShapeD...  39.2 us
    unnamed x11, local copies, waits for them, and re-layouts  5.48 us

profile of v2, /device:TPU:1, one launch (start us, length us, event | category | flops | bytes accessed | tf_op | source)
XLA Modules:
  0.0 44.7 jit_solution(17365233722404931027)
XLA Ops:
  0.0 0.0 copy-start
  0.0 1.6 %copy-done = bf16[128,8192]{1,0:T(8,128)(2,1)S(1)} copy-done((bf16[128,8192]{1,0:T(8,128)(2,1)S(1)}, bf16[128,8192]{1,0:T(8,128)(2,1)}, u32[]{:S(2)}) %copy-start) | copy-done | bytes 2097176
  1.6 0.0 copy-start.1
  1.6 0.9 %copy-done.1 = bf16[128,1024]{1,0:T(8,128)(2,1)S(1)} copy-done((bf16[128,1024]{1,0:T(8,128)(2,1)S(1)}, bf16[128,1024]{1,0:T(8,128)(2,1)}, u32[]{:S(2)}) %copy-start.1) | copy-done | bytes 262168
  2.5 0.0 copy-start.2
  2.5 0.9 %copy-done.2 = bf16[256,256]{1,0:T(8,128)(2,1)S(1)} copy-done((bf16[256,256]{1,0:T(8,128)(2,1)S(1)}, bf16[256,256]{1,0:T(8,128)(2,1)}, u32[]{:S(2)}) %copy-start.2) | copy-done | bytes 131096
  3.4 0.0 copy-start.3
  3.4 0.7 %copy-done.3 = s32[1,512]{1,0:T(1,128)S(1)} copy-done((s32[1,512]{1,0:T(1,128)S(1)}, s32[1,512]{1,0:T(1,128)}, u32[]{:S(2)}) %copy-start.3) | copy-done | bytes 2072
  4.1 0.0 copy-start.4
  4.1 0.7 %copy-done.4 = s32[128]{0:T(128)S(1)} copy-done((s32[128]{0:T(128)S(1)}, s32[128]{0:T(128)}, u32[]{:S(2)}) %copy-start.4) | copy-done | bytes 536
  4.8 39.2 %shard_map.55 = bf16[128,1024]{1,0:T(8,128)(2,1)S(1)} custom-call(bf16[128,8192]{1,0:T(8,128)(2,1)S(1)} %copy-done, bf16[128,1024]{1,0:T(8,128)(2,1)S(1)} %copy-done.1, bf16[256,256]{1,0:T(8,128)(2,1)S(1)} %copy-done.2, s32[1,128]{1,0:T(1,128)S(1)} %bitcast.1, s32[1,512]{1,0:T(1,128)S(1)} %copy-done.3), custom_call_target="tpu_custom_call" | custom-call | tf_op jit(solution)/shard_map/pallas_call | solution.py:394
  44.0 0.7 %copy.7 = bf16[128,1024]{1,0:T(8,128)(2,1)} copy(bf16[128,1024]{1,0:T(8,128)(2,1)S(1)} %shard_map.55) | data formatting | bytes 524288
Async XLA Ops:
  0.0 1.6 %copy-start = (bf16[128,8192]{1,0:T(8,128)(2,1)S(1)}, bf16[128,8192]{1,0:T(8,128)(2,1)}, u32[]{:S(2)}) copy-start(bf16[128,8192]{1,0:T(8,128)(2,1)} %hid_hbm.1) | copy-start | bytes 6291460
  1.6 0.9 %copy-start.1 = (bf16[128,1024]{1,0:T(8,128)(2,1)S(1)}, bf16[128,1024]{1,0:T(8,128)(2,1)}, u32[]{:S(2)}) copy-start(bf16[128,1024]{1,0:T(8,128)(2,1)} %qry_hbm.1) | copy-start | bytes 786436
  2.5 0.9 %copy-start.2 = (bf16[256,256]{1,0:T(8,128)(2,1)S(1)}, bf16[256,256]{1,0:T(8,128)(2,1)}, u32[]{:S(2)}) copy-start(bf16[256,256]{1,0:T(8,128)(2,1)} %w_hbm.1) | copy-start | bytes 393220
  3.4 0.7 %copy-start.3 = (s32[1,512]{1,0:T(1,128)S(1)}, s32[1,512]{1,0:T(1,128)}, u32[]{:S(2)}) copy-start(s32[1,512]{1,0:T(1,128)} %seg_ref.1) | copy-start | bytes 6148
  4.1 0.7 %copy-start.4 = (s32[128]{0:T(128)S(1)}, s32[128]{0:T(128)}, u32[]{:S(2)}) copy-start(s32[128]{0:T(128)} %param.8) | copy-start | bytes 1540

commit v3 on v2

--- a/solution.py
+++ b/solution.py
@@ -111,7 +111,7 @@
 
 def fused(
     nz, ny, nx, hid_hbm, qry_hbm, w_hbm, dest_ref, seg_ref, out_ref,
-    hid, qry, wbuf, outgoing, received, dest_all, kv_all, packed, bias, acc,
+    hid, qry, wbuf, outgoing, received, dest_all, kv_all, packed, bias, acc, tops, totals, numers,
     load_sem, w_send, w_recv, small_send, dest_recv, qry_recv, kv_recv,
 ):
     rows = hid.shape[0]
@@ -342,7 +342,7 @@
             load_w.wait()
             load_h.wait()
             multiply(mine)
-        if i == 3:
+        if i == 5:
             prepare()
         if 0 <= i - lag_third < last:
             take_third(i - lag_third)
@@ -352,24 +352,50 @@
             take_partner(i - lag_far, True)
 
     kv_all[me] = acc[...].astype(jnp.bfloat16)
-    for i, peer in enumerate(peers):
+    for i, peer in enumerate([lax.rem(x * 2 + j, n_seq) for j in range(2, n_seq)] + [x * 2 + 1 - c]):
         small(kv_all.at[me], kv_all.at[me], kv_recv.at[me], (group, peer), 2 * n_seq + i)
-    wait_small(kv_all, kv_recv)
-
     scale = 1.0 / HEAD**0.5
-    key = kv_all[:, :, :HEAD].reshape(keys, HEAD)
-    value = kv_all[:, :, HEAD:].reshape(keys, HEAD)
-    for h in range(GROUP):
+
+    def attend(h, sources, state):
         cols = pl.ds(h * HEAD, HEAD)
-        scores = lax.dot_general(
-            packed[:, cols], key, (((1,), (1,)), ((), ())), preferred_element_type=jnp.float32
-        )
-        scores = scores * scale + bias[...]
+        parts = []
+        for source in sources:
+            scores = lax.dot_general(
+                packed[:, cols], kv_all[source, :, :HEAD], (((1,), (1,)), ((), ())),
+                preferred_element_type=jnp.float32,
+            )
+            window = pl.ds(pl.multiple_of(source * rows, rows), rows)
+            parts.append(scores * scale + bias[:, window])
+        scores = jnp.concatenate(parts, axis=1)
+        value = jnp.concatenate([kv_all[source, :, HEAD:] for source in sources], axis=0)
         top = jnp.max(scores, axis=1, keepdims=True)
+        if state is not None:
+            top = jnp.maximum(top, state[0])
         weights = jnp.exp(scores - top)
         total = jnp.sum(weights, axis=1, keepdims=True)
         numer = jnp.dot(weights.astype(jnp.bfloat16), value, preferred_element_type=jnp.float32)
-        out_ref[:, cols] = (numer / total).astype(jnp.bfloat16)
+        if state is not None:
+            factor = jnp.exp(state[0] - top)
+            total, numer = total + state[1] * factor, numer + state[2] * factor
+        return top, total, numer
+
+    def wait_kv(source):
+        pltpu.make_async_remote_copy(
+            src_ref=kv_all.at[source], dst_ref=kv_all.at[source], send_sem=small_send.at[0],
+            recv_sem=kv_recv.at[source], device_id=partner, device_id_type=MESH,
+        ).wait_recv()
+
+    near = [me, x * 2 + 1 - c]
+    others = [lax.rem(x * 2 + i, n_seq) for i in range(2, n_seq)]
+    wait_kv(near[1])
+    for h in range(GROUP):
+        top, total, numer = attend(h, near, None)
+        tops[h], totals[h], numers[h] = top, total, numer
+    for source in others:
+        wait_kv(source)
+    for h in range(GROUP):
+        top, total, numer = attend(h, others, (tops[h], totals[h], numers[h]))
+        out_ref[:, pl.ds(h * HEAD, HEAD)] = (numer / total).astype(jnp.bfloat16)
 
     for cond, copy in pending:
         if cond is None:
@@ -407,6 +433,9 @@
             pltpu.VMEM((rows, width_q), bf16),
             pltpu.VMEM((rows, keys), f32),
             pltpu.VMEM((rows, width), f32),
+            pltpu.VMEM((GROUP, rows, 1), f32),
+            pltpu.VMEM((GROUP, rows, 1), f32),
+            pltpu.VMEM((GROUP, rows, HEAD), f32),
             dma((3,)),
             dma((PIECES * (9 + 9 * nz),)),
             dma((blocks, PIECES)),

time: 45 us -> 45.1 us (level)
  no operation moved by 1% of the time
where the time goes in v3:
time: 45.1 us; the launch traced here: 44.8 us
  Pallas kernels  39.3 us (87%)
  local copies, waits for them, and re-layouts  5.48 us (12%)
    pallas_call x1, Pallas kernels, fused_shards(): pl.pallas_call(functools.partial(fused, nz, ny, nx), out_shape=jax.ShapeD...  39.3 us
    unnamed x11, local copies, waits for them, and re-layouts  5.48 us

profile of v3, /device:TPU:1, one launch (start us, length us, event | category | flops | bytes accessed | tf_op | source)
XLA Modules:
  0.0 44.8 jit_solution(2253053749852496736)
XLA Ops:
  0.0 0.0 copy-start
  0.0 1.6 %copy-done = bf16[128,8192]{1,0:T(8,128)(2,1)S(1)} copy-done((bf16[128,8192]{1,0:T(8,128)(2,1)S(1)}, bf16[128,8192]{1,0:T(8,128)(2,1)}, u32[]{:S(2)}) %copy-start) | copy-done | bytes 2097176
  1.6 0.0 copy-start.1
  1.6 0.9 %copy-done.1 = bf16[128,1024]{1,0:T(8,128)(2,1)S(1)} copy-done((bf16[128,1024]{1,0:T(8,128)(2,1)S(1)}, bf16[128,1024]{1,0:T(8,128)(2,1)}, u32[]{:S(2)}) %copy-start.1) | copy-done | bytes 262168
  2.5 0.0 copy-start.2
  2.5 0.9 %copy-done.2 = bf16[256,256]{1,0:T(8,128)(2,1)S(1)} copy-done((bf16[256,256]{1,0:T(8,128)(2,1)S(1)}, bf16[256,256]{1,0:T(8,128)(2,1)}, u32[]{:S(2)}) %copy-start.2) | copy-done | bytes 131096
  3.4 0.0 copy-start.3
  3.4 0.7 %copy-done.3 = s32[1,512]{1,0:T(1,128)S(1)} copy-done((s32[1,512]{1,0:T(1,128)S(1)}, s32[1,512]{1,0:T(1,128)}, u32[]{:S(2)}) %copy-start.3) | copy-done | bytes 2072
  4.1 0.0 copy-start.4
  4.1 0.7 %copy-done.4 = s32[128]{0:T(128)S(1)} copy-done((s32[128]{0:T(128)S(1)}, s32[128]{0:T(128)}, u32[]{:S(2)}) %copy-start.4) | copy-done | bytes 536
  4.8 39.3 %shard_map.55 = bf16[128,1024]{1,0:T(8,128)(2,1)S(1)} custom-call(bf16[128,8192]{1,0:T(8,128)(2,1)S(1)} %copy-done, bf16[128,1024]{1,0:T(8,128)(2,1)S(1)} %copy-done.1, bf16[256,256]{1,0:T(8,128)(2,1)S(1)} %copy-done.2, s32[1,128]{1,0:T(1,128)S(1)} %bitcast.1, s32[1,512]{1,0:T(1,128)S(1)} %copy-done.3), custom_call_target="tpu_custom_call" | custom-call | tf_op jit(solution)/shard_map/pallas_call | solution.py:420
  44.1 0.7 %copy.7 = bf16[128,1024]{1,0:T(8,128)(2,1)} copy(bf16[128,1024]{1,0:T(8,128)(2,1)S(1)} %shard_map.55) | data formatting | bytes 524288
Async XLA Ops:
  0.0 1.6 %copy-start = (bf16[128,8192]{1,0:T(8,128)(2,1)S(1)}, bf16[128,8192]{1,0:T(8,128)(2,1)}, u32[]{:S(2)}) copy-start(bf16[128,8192]{1,0:T(8,128)(2,1)} %hid_hbm.1) | copy-start | bytes 6291460
  1.6 0.9 %copy-start.1 = (bf16[128,1024]{1,0:T(8,128)(2,1)S(1)}, bf16[128,1024]{1,0:T(8,128)(2,1)}, u32[]{:S(2)}) copy-start(bf16[128,1024]{1,0:T(8,128)(2,1)} %qry_hbm.1) | copy-start | bytes 786436
  2.5 0.9 %copy-start.2 = (bf16[256,256]{1,0:T(8,128)(2,1)S(1)}, bf16[256,256]{1,0:T(8,128)(2,1)}, u32[]{:S(2)}) copy-start(bf16[256,256]{1,0:T(8,128)(2,1)} %w_hbm.1) | copy-start | bytes 393220
  3.4 0.7 %copy-start.3 = (s32[1,512]{1,0:T(1,128)S(1)}, s32[1,512]{1,0:T(1,128)}, u32[]{:S(2)}) copy-start(s32[1,512]{1,0:T(1,128)} %seg_ref.1) | copy-start | bytes 6148
  4.1 0.7 %copy-start.4 = (s32[128]{0:T(128)S(1)}, s32[128]{0:T(128)}, u32[]{:S(2)}) copy-start(s32[128]{0:T(128)} %param.8) | copy-start | bytes 1540
